TPU v7x, 32 devices: a whole 2x2x4 slice. The times are simulated.
32 devices in a mesh: groups: 2 (over y), dp: 8 (over z, x), section: 2 (over core).
Axes of the slice: x: 2, y: 2, z: 4, core: 2. Of those that a mesh axis runs over, the one named last changes fastest.
Arguments:
- latents: bfloat16 [2048, 3072], P(('groups', 'dp')), parts along dimension 0, may hold values from -6 to 6
- out_grad: float32 [2048, 3072], P(('groups', 'dp')), parts along dimension 0, may hold values from -0.3 to 0.3
- frozen_weight: bfloat16 [2, 3072, 1536], P('section', 'dp'), may hold values from -0.109375 to 0.109375
- norm_gain: float32 [2, 3072], P('section'), may hold values from 0.5 to 1.5
- time_gate: float32 [2, 50], P('section'), may hold values from 0.5 to 2
- down_factors: bfloat16 [2, 96, 64, 3072], P('section', ('groups', 'dp')), parts along dimension 1, may hold values from -0.109375 to 0.109375
- up_factors: bfloat16 [2, 96, 64, 1536], P('section', ('groups', 'dp')), parts along dimension 1, may hold values from -0.75 to 0.75
- block_jobs: int32 [16], P('groups'), parts along dimension 0, may hold values from 0 to 47
- owners: int32 [96], P('groups'), parts along dimension 0, may hold values from 0 to 47, as said below
- block_steps: int32 [16], P(('groups', 'dp')), parts along dimension 0, may hold values from 0 to 49
- block_fill: int32 [16], P(('groups', 'dp')), parts along dimension 0, may hold values from 1 to 128, as said below
Outputs:
- grad_down: float32 [2, 96, 64, 3072], P('section', ('groups', 'dp')), parts along dimension 1
- grad_up: float32 [2, 96, 64, 1536], P('section', ('groups', 'dp')), parts along dimension 1
There are 2 independent parts, one for each index of `groups`. A program takes and returns all parts, laid end to end along the dimension named above; an argument that names none is the same for every part. Nothing has to cross between parts.
Inputs may be any that keep to these rules, and one draw needn't show every extreme that they name: `owners`: no two adapters share a slot; slot 0 and the last slot always hold one. `block_fill`: the live rows come first in their block; in every draw some block is full and some holds a single live row.
All inputs are finite; a program needn't handle non-finite values.
Results may differ from a plain program's by a relative error of at most 0.006.
Values may be sent and summed in bfloat16 or wider, within the bound.
No kernel may reach another device: no remote copies, remote signals or barrier semaphores. Data moves between devices by JAX's collectives and lax.ppermute only.
A program may use at most 128 MiB of HBM per device.

v0:
```python
import jax
import jax.numpy as jnp
from jax import lax
from jax.sharding import PartitionSpec as P

epsilon = 1e-06


def passed_along(value, axis, steps):
    count = lax.axis_size(axis)
    leading, last = (max(0, -steps), min(count, count - steps))
    return lax.ppermute(value, axis, [(source, source + steps) for source in range(leading, last)])


def matrix_product(spec, left_op, right_op):
    return jnp.einsum(spec, left_op, right_op, preferred_element_type=jnp.float32)


def forward_pass(inputs, frozen_layer, gain_row, down_projection_block, up_block, scales):
    out_width = up_block.shape[2]
    block_total, row_count, model_width = inputs.shape
    values = inputs.astype(jnp.float32)
    inverse = lax.rsqrt(jnp.mean(values * values, axis=2) + epsilon)
    normalized_input = (values * inverse[:, :, None] * gain_row).astype(jnp.bfloat16)
    frozen_out = jnp.dot(
        normalized_input.reshape(block_total * row_count, model_width),
        frozen_layer,
        preferred_element_type=jnp.float32,
    )
    frozen_out = frozen_out.reshape(block_total, row_count, out_width)
    reduced_features = matrix_product(
        "uyi,uoi->uyo", normalized_input, down_projection_block
    ).astype(jnp.bfloat16)
    extra = matrix_product("bmq,bqh->bmh", reduced_features, up_block)
    update = scales[:, None, None] * (frozen_out + extra)
    window_out = (values[:, :, :out_width] + update).astype(jnp.bfloat16)
    outputs = jnp.concatenate([window_out, inputs[:, :, out_width:]], axis=2)
    return (outputs, (inputs, normalized_input, inverse, reduced_features))


def backward_pass(
    stored, cotangent, frozen_layer, gain_row, down_projection_block, up_block, scales
):
    inputs, normalized_input, inverse, reduced_features = stored
    out_width = up_block.shape[2]
    block_total, row_count, model_width = inputs.shape
    values = inputs.astype(jnp.float32)
    delta_output = (scales[:, None, None] * cotangent[:, :, :out_width]).astype(jnp.bfloat16)
    grad_upper = matrix_product("bmq,bmh->bqh", reduced_features, delta_output)
    low_rank_delta = matrix_product("bmh,bqh->bmq", delta_output, up_block).astype(jnp.bfloat16)
    lower_gradient = matrix_product("hoc,hou->hcu", low_rank_delta, normalized_input)
    through = lax.dot_general(
        delta_output.reshape(block_total * row_count, out_width),
        frozen_layer,
        (((1,), (1,)), ((), ())),
        preferred_element_type=jnp.float32,
    )
    delta_normalized = through.reshape(block_total, row_count, model_width) + matrix_product(
        "rha,rak->rhk", low_rank_delta, down_projection_block
    )
    scaled = gain_row * delta_normalized
    inner = jnp.mean(values * scaled, axis=2)
    cubed = inverse * inverse * inverse
    delta_in = inverse[:, :, None] * scaled - values * (cubed * inner)[:, :, None]
    carried = (cotangent + delta_in).astype(jnp.bfloat16)
    return (carried, lower_gradient, grad_upper)


def body(
    latents,
    out_grad,
    frozen_weight,
    norm_gain,
    time_gate,
    down_factors,
    up_factors,
    block_jobs,
    owners,
    block_steps,
    block_fill,
):
    position = lax.axis_index("section")
    lane_count = lax.axis_size("dp")
    slot_local = down_factors.shape[1]
    low_rank = down_factors.shape[2]
    model_width = down_factors.shape[3]
    blocks_dev = block_fill.shape[0]
    block_rows = latents.shape[0] // blocks_dev
    is_first = position == 0
    frozen_layer = lax.all_gather(frozen_weight[0], "dp", axis=0, tiled=True)
    gain_row = norm_gain[0]
    gate_row = time_gate[0]
    chosen = block_steps[:, None] == jnp.arange(gate_row.shape[0], dtype=jnp.int32)[None, :]
    scales = jnp.sum(jnp.where(chosen, gate_row[None, :], 0.0), axis=1)
    matches = block_jobs[:, None] == jnp.arange(owners.shape[0], dtype=jnp.int32)[None, :]
    slot_of = jnp.sum(jnp.where(matches, owners[None, :], 0), axis=1)
    spread_down, spread_up = (
        lax.all_to_all(down_factors[0], "dp", split_axis=2, concat_axis=0, tiled=True),
        lax.all_to_all(up_factors[0], "dp", split_axis=2, concat_axis=0, tiled=True),
    )
    down_projection_block, up_block = (
        lax.all_to_all(spread_down[slot_of], "dp", split_axis=0, concat_axis=2, tiled=True),
        lax.all_to_all(spread_up[slot_of], "dp", split_axis=0, concat_axis=2, tiled=True),
    )
    micro_count = 1
    micro_rows = block_rows // micro_count
    block_view = latents.reshape(blocks_dev, block_rows, model_width)
    live_rows = jnp.arange(block_rows, dtype=jnp.int32)[None, :] < block_fill[:, None]
    masked = jnp.where(
        live_rows[:, :, None], out_grad.reshape(blocks_dev, block_rows, model_width), 0.0
    )
    incoming = jnp.zeros((blocks_dev, micro_rows, model_width), jnp.bfloat16)
    kept = []
    for turn_index in range(micro_count + 1):
        source = jnp.where(is_first, block_view, incoming)
        outputs, stored = forward_pass(
            source, frozen_layer, gain_row, down_projection_block, up_block, scales
        )
        kept.append(stored)
        if turn_index < micro_count:
            incoming = passed_along(outputs, "section", 1)
    states = [
        jax.tree.map(lambda former, latter: jnp.where(is_first, former, latter), kept[0], kept[1])
    ]
    returned = jnp.zeros((blocks_dev, micro_rows, model_width), jnp.bfloat16)
    sum_down = jnp.zeros((blocks_dev, low_rank, model_width), jnp.float32)
    sum_up = jnp.zeros((blocks_dev, low_rank, up_block.shape[2]), jnp.float32)
    for turn_index in range(micro_count + 1):
        late_micro = min(turn_index, micro_count - 1)
        early_micro = max(turn_index - 1, 0)
        current = jax.tree.map(
            lambda former, latter: jnp.where(is_first, former, latter),
            states[early_micro],
            states[late_micro],
        )
        cotangent = jnp.where(is_first, returned.astype(jnp.float32), masked)
        carried, lower_gradient, grad_upper = backward_pass(
            current, cotangent, frozen_layer, gain_row, down_projection_block, up_block, scales
        )
        useful = jnp.where(is_first, turn_index >= 1, turn_index < micro_count)
        sum_down = sum_down + jnp.where(useful, lower_gradient, 0.0)
        sum_up = sum_up + jnp.where(useful, grad_upper, 0.0)
        if turn_index < micro_count:
            returned = passed_along(carried, "section", -1)
    pieces_down, pieces_up = (
        lax.all_to_all(sum_down, "dp", split_axis=2, concat_axis=0, tiled=True),
        lax.all_to_all(sum_up, "dp", split_axis=2, concat_axis=0, tiled=True),
    )
    slot_total = lane_count * slot_local
    onehot = (jnp.arange(slot_total, dtype=jnp.int32)[:, None] == slot_of[None, :]).astype(
        jnp.float32
    )
    block_total = pieces_down.shape[0]
    slot_down = jnp.dot(
        onehot,
        pieces_down.reshape(block_total, -1),
        precision=lax.Precision.HIGHEST,
        preferred_element_type=jnp.float32,
    )
    slot_up = jnp.dot(
        onehot,
        pieces_up.reshape(block_total, -1),
        precision=lax.Precision.HIGHEST,
        preferred_element_type=jnp.float32,
    )
    slot_down = slot_down.reshape(slot_total, low_rank, pieces_down.shape[2])
    slot_up = slot_up.reshape(slot_total, low_rank, pieces_up.shape[2])
    owned_down, owned_up = (
        lax.all_to_all(slot_down, "dp", split_axis=0, concat_axis=2, tiled=True),
        lax.all_to_all(slot_up, "dp", split_axis=0, concat_axis=2, tiled=True),
    )
    return (owned_down[None], owned_up[None])


def solution(mesh):
    placed = (
        P(("groups", "dp"), None),
        P(("groups", "dp"), None),
        P("section", "dp", None),
        P("section", None),
        P("section", None),
        P("section", ("groups", "dp"), None, None),
        P("section", ("groups", "dp"), None, None),
        P("groups"),
        P("groups"),
        P(("groups", "dp")),
        P(("groups", "dp")),
    )
    return jax.shard_map(
        body,
        mesh=mesh,
        in_specs=placed,
        out_specs=(
            P("section", ("groups", "dp"), None, None),
            P("section", ("groups", "dp"), None, None),
        ),
        check_vma=False,
    )
```

profile of v0, /device:TPU:0, one launch (start us, length us, event | category | flops | bytes accessed | tf_op | source)
XLA Modules:
  0.0 537.3 jit_solution(2931471331591064361)
XLA Ops:
  8.4 3.4 copy.64
  11.9 2.0 bitcast_bitcast_fusion.1
  13.9 3.1 reshape.236
  17.0 7.5 %all-to-all-start = ((bf16[8,2,36864]{2,1,0:T(2,128)(2,1)}), bf16[8,2,36864]{2,1,0:T(2,128)(2,1)S(1)}, u32[]{:S(2)}, u32[]{:S(2)}) async-start(bf16[8,2,36864]{2,1,0:T(2,128)(2,1)} %reshape.236), calls=%async_computation | async-start | bytes 2359296 | tf_op jit(solution)/shard_map/all_to_all | solution.py:99
  24.5 6.0 %copy.68 = bf16[1,6,64,3072]{2,1,3,0:T(8,128)(2,1)} copy(bf16[1,6,64,3072]{3,2,1,0:T(8,128)(2,1)S(1)} %copy-done.7) | data formatting | bytes 4718592 | tf_op args[5]
  30.5 6.4 %bitcast_bitcast_fusion = bf16[3072,6,64]{2,1,0:T(8,128)(2,1)} fusion(bf16[1,6,64,3072]{2,1,3,0:T(8,128)(2,1)} %copy.68), kind=kLoop, calls=%fused_computation.81 | loop fusion | bytes 4718592
  37.0 8.5 %reshape.238 = bf16[8,2,73728]{2,1,0:T(2,128)(2,1)} reshape(bf16[3072,6,64]{2,1,0:T(8,128)(2,1)} %bitcast_bitcast_fusion) | data formatting | bytes 4718592
  45.5 38.7 %all-to-all-done = bf16[8,2,36864]{2,1,0:T(2,128)(2,1)S(1)} async-done(((bf16[8,2,36864]{2,1,0:T(2,128)(2,1)}), bf16[8,2,36864]{2,1,0:T(2,128)(2,1)S(1)}, u32[]{:S(2)}, u32[]{:S(2)}) %all-to-all-start) | async-done | bytes 1179680 | tf_op jit(solution)/shard_map/all_to_all | solution.py:99
  84.2 1.0 copy-done.3
  85.2 4.4 all-to-all-start.2
  91.0 2.1 select_bitcast_fusion
  93.1 3.6 reshape.237
  96.6 2.7 copy.66
  99.3 2.7 gather_fusion
  102.1 98.8 %all-to-all-done.2 = bf16[8,2,73728]{2,1,0:T(2,128)(2,1)} async-done(((bf16[8,2,73728]{2,1,0:T(2,128)(2,1)}), bf16[8,2,73728]{2,1,0:T(2,128)(2,1)}, u32[]{:S(2)}, u32[]{:S(2)}) %all-to-all-start.2) | async-done | bytes 2359328 | tf_op jit(solution)/shard_map/all_to_all | solution.py:98
  200.9 9.0 %all-to-all-start.1 = ((bf16[8,64,192]{2,1,0:T(8,128)(2,1)}), bf16[8,64,192]{2,1,0:T(8,128)(2,1)S(1)}, u32[]{:S(2)}, u32[]{:S(2)}) async-start(bf16[8,64,192]{2,1,0:T(8,128)(2,1)} %gather_fusion), calls=%async_computation.1 | async-start | bytes 524288 | tf_op jit(solution)/shard_map/all_to_all | solution.py:103
  210.0 1.3 convert_bitcast_fusion
  212.0 0.8 slice.22
  213.6 8.2 %reshape.239 = bf16[3072,6,64]{2,1,0:T(8,128)(2,1)} reshape(bf16[8,2,73728]{2,1,0:T(2,128)(2,1)} %all-to-all-done.2) | data formatting | bytes 4718592
  221.9 6.7 %copy.70 = bf16[8,6,64,384]{3,2,1,0:T(8,128)(2,1)} copy(bf16[8,6,64,384]{2,1,3,0:T(8,128)(2,1)} %bitcast.151) | data formatting | bytes 4718592 | tf_op jit(solution)/shard_map/all_to_all | solution.py:98
  228.5 3.1 gather_fusion.1
  231.7 6.0 %all-to-all-start.3 = ((bf16[8,64,384]{2,1,0:T(8,128)(2,1)}), bf16[8,64,384]{2,1,0:T(8,128)(2,1)S(1)}, u32[]{:S(2)}, u32[]{:S(2)}) async-start(bf16[8,64,384]{2,1,0:T(8,128)(2,1)} %gather_fusion.1), calls=%async_computation.3 | async-start | bytes 786432 | tf_op jit(solution)/shard_map/all_to_all | solution.py:102
  238.3 1.8 copy.67
  240.1 1.2 reshape.210
  241.3 7.4 %all-to-all-done.3 = bf16[8,64,384]{2,1,0:T(8,128)(2,1)S(1)} async-done(((bf16[8,64,384]{2,1,0:T(8,128)(2,1)}), bf16[8,64,384]{2,1,0:T(8,128)(2,1)S(1)}, u32[]{:S(2)}, u32[]{:S(2)}) %all-to-all-start.3) | async-done | bytes 393248 | tf_op jit(solution)/shard_map/all_to_all | solution.py:102
  248.8 0.7 copy-done.11
  250.1 5.3 fusion.2
  255.4 1.4 fusion.10
  257.0 1.3 collective-permute-start
  258.7 3.1 fusion
  261.8 0.8 fusion.16
  263.2 1.4 fusion.19
  264.7 1.6 collective-permute-start.1
  266.3 1.5 fusion.23
  267.7 1.6 collective-permute-done.1
  269.3 1.6 fusion.34
  272.9 7.1 %reduce.7 = f32[1536,64]{1,0:T(8,128)S(1)} reduce(f32[1536,1,64]{2,1,0:T(1,128)S(1)} %bitcast.157, f32[]{:T(128)} %broadcast.202), dimensions={1}, to_apply=%bitcast.124.reduce_sub_computation | reduce | bytes 786436
  280.0 1.2 reshape.242
  281.3 4.1 all-to-all-start.6
  285.4 1.7 convolution_select_fusion
  287.1 1.8 fusion.6
  288.9 1.7 copy.72
  290.6 13.6 %reduce.5 = f32[3072,64]{1,0:T(8,128)S(1)} reduce(f32[3072,1,64]{2,1,0:T(1,128)S(1)} %bitcast.155, f32[]{:T(128)} %broadcast.202), dimensions={1}, to_apply=%bitcast.122.reduce_sub_computation | reduce | bytes 1572868
  304.2 1.9 reshape.240
  306.0 6.1 %all-to-all-start.4 = ((f32[8,1,24576]{2,1,0:T(1,128)}), f32[8,1,24576]{2,1,0:T(1,128)S(1)}, u32[]{:S(2)}, u32[]{:S(2)}) async-start(f32[8,1,24576]{2,1,0:T(1,128)} %reshape.240), calls=%async_computation.4 | async-start | bytes 1572864 | tf_op jit(solution)/shard_map/all_to_all | solution.py:146
  312.2 2.5 reduce.8
  314.7 1.0 reshape.243
  316.5 1.5 fusion.30
  318.0 3.5 copy.79
  321.5 11.2 %all-to-all-done.4 = f32[8,1,24576]{2,1,0:T(1,128)S(1)} async-done(((f32[8,1,24576]{2,1,0:T(1,128)}), f32[8,1,24576]{2,1,0:T(1,128)S(1)}, u32[]{:S(2)}, u32[]{:S(2)}) %all-to-all-start.4) | async-done | bytes 786464 | tf_op jit(solution)/shard_map/all_to_all | solution.py:146
  332.7 0.9 copy-done.6
  333.5 3.9 all-to-all-start.7
  337.5 4.4 reduce.6
  341.9 4.2 reshape.241
  346.2 2.7 copy.73
  348.9 3.3 fusion.37
  352.2 3.6 copy.74
  355.8 52.5 %all-to-all-done.7 = f32[48,64,192]{2,1,0:T(8,128)S(1)} async-done(((f32[48,64,192]{2,1,0:T(8,128)}), f32[48,64,192]{2,1,0:T(8,128)S(1)}, u32[]{:S(2)}, u32[]{:S(2)}) %all-to-all-start.7) | async-done | bytes 2359328 | tf_op jit(solution)/shard_map/all_to_all | solution.py:170
  408.3 4.9 all-to-all-start.5
  413.2 3.5 copy.80
  416.7 4.3 broadcast_in_dim.68
  421.0 96.0 %all-to-all-done.5 = f32[48,64,384]{2,1,0:T(8,128)} async-done(((f32[48,64,384]{2,1,0:T(8,128)}), f32[48,64,384]{2,1,0:T(8,128)}, u32[]{:S(2)}, u32[]{:S(2)}) %all-to-all-start.5) | async-done | bytes 4718624 | tf_op jit(solution)/shard_map/all_to_all | solution.py:169
  517.0 7.2 %copy.75 = f32[6,64,8,384]{3,2,1,0:T(8,128)} copy(f32[6,64,8,384]{3,1,0,2:T(8,128)} %bitcast.39) | data formatting | bytes 9437184 | tf_op jit(solution)/shard_map/all_to_all | solution.py:169
  524.2 5.8 %broadcast_in_dim.66 = f32[1,6,64,3072]{3,2,1,0:T(8,128)} reshape(f32[6,64,8,384]{3,2,1,0:T(8,128)} %copy.75) | data formatting | bytes 9437184 | tf_op jit(solution)/shard_map/broadcast_in_dim | solution.py:172
  (87 shorter events, 7.8 us)
Async XLA Ops:
  7.2 1.3 copy-start.16
  7.2 242.9 %all-gather.3.cloned.1.call-start = ((), (), s32[]{:S(2)}) async-start(), calls=%async_computation.8 | async-start | bytes 10616832 | tf_op jit(solution)/shard_map/all_gather | solution.py:90
  17.0 7.5 %copy-start.7 = (bf16[1,6,64,3072]{3,2,1,0:T(8,128)(2,1)S(1)}, bf16[1,6,64,3072]{3,2,1,0:T(8,128)(2,1)}, u32[]{:S(2)}) copy-start(bf16[1,6,64,3072]{3,2,1,0:T(8,128)(2,1)} %param.16) | copy-start | bytes 7077892
  17.0 67.2 %all-to-all-start = ((bf16[8,2,36864]{2,1,0:T(2,128)(2,1)}), bf16[8,2,36864]{2,1,0:T(2,128)(2,1)S(1)}, u32[]{:S(2)}, u32[]{:S(2)}) async-start(bf16[8,2,36864]{2,1,0:T(2,128)(2,1)} %reshape.236), calls=%async_computation | async-start | bytes 2359296 | tf_op jit(solution)/shard_map/all_to_all | solution.py:99
  45.5 44.7 %copy-start.27 = (s32[48]{0:T(128)S(1)}, s32[48]{0:T(128)}, u32[]{:S(2)}) copy-start(s32[48]{0:T(128)} %param.19) | copy-start | bytes 580
  45.5 44.8 %copy-start.28 = (s32[8]{0:T(128)S(1)}, s32[8]{0:T(128)}, u32[]{:S(2)}) copy-start(s32[8]{0:T(128)} %param.18) | copy-start | bytes 100
  45.5 45.5 %copy-start.10 = (f32[128,3072]{1,0:T(8,128)S(1)}, f32[128,3072]{1,0:T(8,128)}, u32[]{:S(2)}) copy-start(f32[128,3072]{1,0:T(8,128)} %param.12) | copy-start | bytes 4718596
  84.2 1.0 copy-start.3
  85.2 115.8 %all-to-all-start.2 = ((bf16[8,2,73728]{2,1,0:T(2,128)(2,1)}), bf16[8,2,73728]{2,1,0:T(2,128)(2,1)}, u32[]{:S(2)}, u32[]{:S(2)}) async-start(bf16[8,2,73728]{2,1,0:T(2,128)(2,1)} %reshape.238), calls=%async_computation.2 | async-start | bytes 4718592 | tf_op jit(solution)/shard_map/all_to_all | solution.py:98
  90.4 0.5 copy-start.24
  99.3 110.6 %copy-start = (bf16[128,3072]{1,0:T(8,128)(2,1)S(1)}, bf16[128,3072]{1,0:T(8,128)(2,1)}, u32[]{:S(2)}) copy-start(bf16[128,3072]{1,0:T(8,128)(2,1)} %param.11) | copy-start | bytes 2359300
  200.9 30.7 %all-to-all-start.1 = ((bf16[8,64,192]{2,1,0:T(8,128)(2,1)}), bf16[8,64,192]{2,1,0:T(8,128)(2,1)S(1)}, u32[]{:S(2)}, u32[]{:S(2)}) async-start(bf16[8,64,192]{2,1,0:T(8,128)(2,1)} %gather_fusion), calls=%async_computation.1 | async-start | bytes 524288 | tf_op jit(solution)/shard_map/all_to_all | solution.py:103
  210.0 2.8 copy-start.29
  213.6 24.0 %copy-start.22 = (f32[128]{0:T(128)}, f32[128]{0:T(128)S(1)}, u32[]{:S(2)}) copy-start(f32[128]{0:T(128)S(1)} %fusion.20) | copy-start | bytes 1540
  228.5 9.2 %copy-start.1 = (f32[1,128,3072]{2,1,0:T(8,128)S(1)}, f32[1,128,3072]{2,1,0:T(8,128)}, u32[]{:S(2)}) copy-start(f32[1,128,3072]{2,1,0:T(8,128)} %get-tuple-element.7) | copy-start | bytes 4718596
  231.7 6.0 %copy-start.17 = (bf16[8,64,192]{2,1,0:T(8,128)(2,1)}, bf16[8,64,192]{2,1,0:T(8,128)(2,1)S(1)}, u32[]{:S(2)}) copy-start(bf16[8,64,192]{2,1,0:T(8,128)(2,1)S(1)} %all-to-all-done.1) | copy-start | bytes 589828
  231.7 17.1 %all-to-all-start.3 = ((bf16[8,64,384]{2,1,0:T(8,128)(2,1)}), bf16[8,64,384]{2,1,0:T(8,128)(2,1)S(1)}, u32[]{:S(2)}, u32[]{:S(2)}) async-start(bf16[8,64,384]{2,1,0:T(8,128)(2,1)} %gather_fusion.1), calls=%async_computation.3 | async-start | bytes 786432 | tf_op jit(solution)/shard_map/all_to_all | solution.py:102
  237.7 11.9 %copy-start.19 = (f32[1,3072]{1,0:T(1,128)S(1)}, f32[1,3072]{1,0:T(1,128)}, u32[]{:S(2)}) copy-start(f32[1,3072]{1,0:T(1,128)} %param.14) | copy-start | bytes 36868
  237.7 12.4 %copy-start.30 = (f32[128]{0:T(128)}, f32[128]{0:T(128)S(1)}, u32[]{:S(2)}) copy-start(f32[128]{0:T(128)S(1)} %add_rsqrt_fusion.1) | copy-start | bytes 1540
  241.3 17.0 %copy-start.8 = (bf16[64,1536]{1,0:T(8,128)(2,1)}, bf16[64,1536]{1,0:T(8,128)(2,1)S(1)}, u32[]{:S(2)}) copy-start(bf16[64,1536]{1,0:T(8,128)(2,1)S(1)} %reshape.210) | copy-start | bytes 589828
  248.8 0.7 copy-start.11
  250.1 5.4 copy-start.18
  250.1 5.3 copy-start.5
  250.1 8.5 %copy-start.2 = (bf16[1,3072,1536]{2,1,0:T(8,128)(2,1)S(1)}, bf16[1,3072,1536]{2,1,0:T(8,128)(2,1)}, u32[]{:S(2)}) copy-start(bf16[1,3072,1536]{2,1,0:T(8,128)(2,1)} %all-gather.3.cloned.1.call-done) | copy-start | bytes 28311556
  255.4 1.5 copy-start.13
  257.0 4.7 collective-permute-start
  258.6 3.1 copy-start.12
  258.7 3.1 copy-start.20
  261.8 0.9 copy-start.23
  264.7 4.6 copy-start.4
  264.7 4.6 collective-permute-start.1
  271.0 0.7 copy-start.14
  272.9 12.5 %copy-start.9 = (bf16[64,1536]{1,0:T(8,128)(2,1)S(1)}, bf16[64,1536]{1,0:T(8,128)(2,1)}, u32[]{:S(2)}) copy-start(bf16[64,1536]{1,0:T(8,128)(2,1)} %copy-done.8) | copy-start | bytes 589828
  272.9 12.5 %copy-start.21 = (f32[1,3072]{1,0:T(1,128)S(1)}, f32[1,3072]{1,0:T(1,128)}, u32[]{:S(2)}) copy-start(f32[1,3072]{1,0:T(1,128)} %param.14) | copy-start | bytes 36868
  272.9 12.5 %copy-start.26 = (f32[128]{0:T(128)S(1)}, f32[128]{0:T(128)}, u32[]{:S(2)}) copy-start(f32[128]{0:T(128)} %get-tuple-element.11) | copy-start | bytes 1540
  272.9 12.5 %copy-start.31 = (f32[128]{0:T(128)S(1)}, f32[128]{0:T(128)}, u32[]{:S(2)}) copy-start(f32[128]{0:T(128)} %copy-done.30) | copy-start | bytes 1540
  280.0 5.4 %copy-start.15 = (bf16[128,1536]{1,0:T(8,128)(2,1)S(1)}, bf16[128,1536]{1,0:T(8,128)(2,1)}, u32[]{:S(2)}) copy-start(bf16[128,1536]{1,0:T(8,128)(2,1)} %copy-done.14) | copy-start | bytes 1179652
  281.3 24.8 %all-to-all-start.6 = ((f32[8,1,12288]{2,1,0:T(1,128)}), f32[8,1,12288]{2,1,0:T(1,128)}, u32[]{:S(2)}, u32[]{:S(2)}) async-start(f32[8,1,12288]{2,1,0:T(1,128)} %reshape.242), calls=%async_computation.6 | async-start | bytes 786432 | tf_op jit(solution)/shard_map/all_to_all | solution.py:147
  306.0 26.6 %all-to-all-start.4 = ((f32[8,1,24576]{2,1,0:T(1,128)}), f32[8,1,24576]{2,1,0:T(1,128)S(1)}, u32[]{:S(2)}, u32[]{:S(2)}) async-start(f32[8,1,24576]{2,1,0:T(1,128)} %reshape.240), calls=%async_computation.4 | async-start | bytes 1572864 | tf_op jit(solution)/shard_map/all_to_all | solution.py:146
  315.7 0.8 copy-start.25
  332.6 0.9 copy-start.6
  333.5 74.8 %all-to-all-start.7 = ((f32[48,64,192]{2,1,0:T(8,128)}), f32[48,64,192]{2,1,0:T(8,128)S(1)}, u32[]{:S(2)}, u32[]{:S(2)}) async-start(f32[48,64,192]{2,1,0:T(8,128)} %copy.79), calls=%async_computation.7 | async-start | bytes 6291456 | tf_op jit(solution)/shard_map/all_to_all | solution.py:170
  408.3 108.7 %all-to-all-start.5 = ((f32[48,64,384]{2,1,0:T(8,128)}), f32[48,64,384]{2,1,0:T(8,128)}, u32[]{:S(2)}, u32[]{:S(2)}) async-start(f32[48,64,384]{2,1,0:T(8,128)} %copy.74), calls=%async_computation.5 | async-start | bytes 9437184 | tf_op jit(solution)/shard_map/all_to_all | solution.py:169
Sparse Core Ops, SparseCore 0:
  10.2 214.9 all-gather.2
where the time goes:
time: 547 us; the launch traced here: 537 us
  waiting for transfers between devices  307 us (56%)
  local copies, waits for them, and re-layouts  107 us (20%)
  starting transfers between devices  48.9 us (9%)
  other arithmetic  36.5 us (7%)
  matrix products  21.4 us (4%)
  between operations  16.4 us (3%)
    all_to_all x1, waiting for transfers between devices, body(): lax.all_to_all(down_factors[0], 'dp', split_axis=2, concat_axis=0, tiled=...  98.8 us
    all_to_all x1, waiting for transfers between devices, body(): lax.all_to_all(slot_down, 'dp', split_axis=0, concat_axis=2, tiled=True)  96 us
    unnamed x78, local copies, waits for them, and re-layouts  54.6 us
    all_to_all x1, waiting for transfers between devices, body(): lax.all_to_all(slot_up, 'dp', split_axis=0, concat_axis=2, tiled=True)  52.5 us
    all_to_all x1, waiting for transfers between devices, body(): lax.all_to_all(up_factors[0], 'dp', split_axis=2, concat_axis=0, tiled=True)  38.7 us
    unnamed x2, other arithmetic  20.7 us
    all_to_all x1, waiting for transfers between devices, body(): lax.all_to_all(sum_down, 'dp', split_axis=2, concat_axis=0, tiled=True)  11.2 us
  transfers between devices with their start and end apart: 11, of which 7 were waited for; matrix products, arithmetic and copies ran while one was open for 24% of the time, Pallas kernels for 0%

commit v1 on v0

--- a/solution.py
+++ b/solution.py
@@ -95,7 +95,12 @@
     matches = block_jobs[:, None] == jnp.arange(owners.shape[0], dtype=jnp.int32)[None, :]
     slot_of = jnp.sum(jnp.where(matches, owners[None, :], 0), axis=1)
     spread_down, spread_up = (
-        lax.all_to_all(down_factors[0], "dp", split_axis=2, concat_axis=0, tiled=True),
+        jnp.concatenate(
+            lax.all_to_all(
+                jnp.stack(jnp.split(down_factors[0], lax.axis_size("dp"), axis=2)), "dp", 0, 0
+            ),
+            axis=0,
+        ),
         lax.all_to_all(up_factors[0], "dp", split_axis=2, concat_axis=0, tiled=True),
     )
     down_projection_block, up_block = (

time: 547 us -> 535 us (0.978)
  local copies, waits for them, and re-layouts: 107 us -> 76.9 us
  waiting for transfers between devices: 307 us -> 328 us
    unnamed x78 -> x81, local copies, waits for them, and re-layouts: 54.6 us -> 30.5 us
    all_to_all x1, waiting for transfers between devices: 38.7 us -> 53.7 us  [body(): lax.all_to_all(up_factors[0], 'dp', split_axis=2, concat_axis=0, tiled=True)]
    all_to_all x1 -> x0, local copies, waits for them, and re-layouts: 6.67 us -> none  [body(): lax.all_to_all(down_factors[0], 'dp', split_axis=2, concat_axis=0, tiled=...]
    all_to_all x1, waiting for transfers between devices: 0.01 us -> 5.92 us  [body(): lax.all_to_all(spread_up[slot_of], 'dp', split_axis=0, concat_axis=2, til...]
  transfers between devices with their start and end apart: 11 -> 11, of which waited for: 7 -> 8; matrix products, arithmetic and copies ran while one was open for 24% -> 18% of each run, Pallas kernels for 0% -> 0%
where the time goes in v1:
time: 535 us; the launch traced here: 526 us
  waiting for transfers between devices  328 us (61%)
  local copies, waits for them, and re-layouts  76.9 us (14%)
  starting transfers between devices  46.7 us (9%)
  other arithmetic  36.9 us (7%)
  matrix products  21.5 us (4%)
  between operations  16.2 us (3%)
    all_to_all x1, waiting for transfers between devices, body(): lax.all_to_all(jnp.stack(jnp.split(down_factors[0], lax.axis_size('dp'),...  98.9 us
    all_to_all x1, waiting for transfers between devices, body(): lax.all_to_all(slot_down, 'dp', split_axis=0, concat_axis=2, tiled=True)  96 us
    all_to_all x1, waiting for transfers between devices, body(): lax.all_to_all(up_factors[0], 'dp', split_axis=2, concat_axis=0, tiled=True)  53.7 us
    all_to_all x1, waiting for transfers between devices, body(): lax.all_to_all(slot_up, 'dp', split_axis=0, concat_axis=2, tiled=True)  52.5 us
    unnamed x81, local copies, waits for them, and re-layouts  30.5 us
    unnamed x2, other arithmetic  20.8 us
    all_to_all x1, waiting for transfers between devices, body(): lax.all_to_all(sum_down, 'dp', split_axis=2, concat_axis=0, tiled=True)  11.2 us
  transfers between devices with their start and end apart: 11, of which 8 were waited for; matrix products, arithmetic and copies ran while one was open for 18% of the time, Pallas kernels for 0%

profile of v1, /device:TPU:0, one launch (start us, length us, event | category | flops | bytes accessed | tf_op | source)
XLA Modules:
  0.0 526.2 jit_solution(17402442675074097662)
XLA Ops:
  8.4 3.4 copy.56
  11.9 2.0 bitcast_bitcast_fusion
  13.9 3.1 reshape.240
  17.0 7.5 %all-to-all-start = ((bf16[8,2,36864]{2,1,0:T(2,128)(2,1)}), bf16[8,2,36864]{2,1,0:T(2,128)(2,1)S(1)}, u32[]{:S(2)}, u32[]{:S(2)}) async-start(bf16[8,2,36864]{2,1,0:T(2,128)(2,1)} %reshape.240), calls=%async_computation | async-start | bytes 2359296 | tf_op jit(solution)/shard_map/all_to_all | solution.py:104
  24.5 0.7 fusion.42
  25.3 0.7 fusion.41
  26.7 0.7 fusion.39
  27.5 0.7 fusion.38
  28.2 0.7 fusion.37
  30.4 53.7 %all-to-all-done = bf16[8,2,36864]{2,1,0:T(2,128)(2,1)S(1)} async-done(((bf16[8,2,36864]{2,1,0:T(2,128)(2,1)}), bf16[8,2,36864]{2,1,0:T(2,128)(2,1)S(1)}, u32[]{:S(2)}, u32[]{:S(2)}) %all-to-all-start) | async-done | bytes 1179680 | tf_op jit(solution)/shard_map/all_to_all | solution.py:104
  84.2 1.0 copy-done.3
  85.2 4.4 all-to-all-start.2
  91.0 2.1 select_bitcast_fusion
  93.1 3.6 reshape.241
  96.6 2.7 copy.58
  99.3 2.8 gather_fusion
  102.1 98.9 %all-to-all-done.2 = bf16[8,6,64,384]{3,2,1,0:T(8,128)(2,1)} async-done(((bf16[8,6,64,384]{3,2,1,0:T(8,128)(2,1)}), bf16[8,6,64,384]{3,2,1,0:T(8,128)(2,1)}, u32[]{:S(2)}, u32[]{:S(2)}) %all-to-all-start.2) | async-done | bytes 2359328 | tf_op jit(solution)/shard_map/all_to_all | solution.py:99
  201.0 9.0 %all-to-all-start.1 = ((bf16[8,64,192]{2,1,0:T(8,128)(2,1)}), bf16[8,64,192]{2,1,0:T(8,128)(2,1)S(1)}, u32[]{:S(2)}, u32[]{:S(2)}) async-start(bf16[8,64,192]{2,1,0:T(8,128)(2,1)} %gather_fusion), calls=%async_computation.1 | async-start | bytes 524288 | tf_op jit(solution)/shard_map/all_to_all | solution.py:108
  210.0 1.3 convert_bitcast_fusion
  212.0 0.8 slice.22
  213.7 3.0 gather_fusion.1
  216.7 5.9 %all-to-all-done.1 = bf16[8,64,192]{2,1,0:T(8,128)(2,1)S(1)} async-done(((bf16[8,64,192]{2,1,0:T(8,128)(2,1)}), bf16[8,64,192]{2,1,0:T(8,128)(2,1)S(1)}, u32[]{:S(2)}, u32[]{:S(2)}) %all-to-all-start.1) | async-done | bytes 196640 | tf_op jit(solution)/shard_map/all_to_all | solution.py:108
  222.6 3.5 all-to-all-start.3
  226.8 1.8 copy.59
  228.6 1.2 reshape.213
  229.8 7.6 %all-to-all-done.3 = bf16[8,64,384]{2,1,0:T(8,128)(2,1)S(1)} async-done(((bf16[8,64,384]{2,1,0:T(8,128)(2,1)}), bf16[8,64,384]{2,1,0:T(8,128)(2,1)S(1)}, u32[]{:S(2)}, u32[]{:S(2)}) %all-to-all-start.3) | async-done | bytes 393248 | tf_op jit(solution)/shard_map/all_to_all | solution.py:107
  238.8 5.3 %fusion.2 = f32[128,1536]{1,0:T(8,128)S(1)} fusion(bf16[1,3072,1536]{2,1,0:T(8,128)(2,1)} %all-gather.3.cloned.1.call-done, f32[3072]{0:T(1024)S(1)} %bitcast.200, f32[128]{0:T(128)S(1)} %add_rsqrt_fusion.1, bf16[128,3072]{1,0:T(8,128)(2,1)S(1)} %copy-done, pred[]{:T(512)S(6)} %eq.53), kind=kOutput, calls=%fused_computation.4 | convolution fusion | flops 1209925632 | bytes 11022849 | tf_op jit(solution)/shard_map/dot_general | solution.py:25
  244.1 1.5 fusion.10
  245.7 1.3 collective-permute-start
  247.3 3.1 fusion
  250.5 0.8 fusion.16
  251.9 1.4 fusion.19
  253.3 1.7 collective-permute-start.1
  255.0 1.5 fusion.23
  256.5 1.4 collective-permute-done.1
  258.0 1.7 fusion.34
  261.6 7.2 %reduce.7 = f32[1536,64]{1,0:T(8,128)S(1)} reduce(f32[1536,1,64]{2,1,0:T(1,128)S(1)} %bitcast.179, f32[]{:T(128)} %broadcast.202), dimensions={1}, to_apply=%bitcast.150.reduce_sub_computation | reduce | bytes 786436
  268.8 1.2 reshape.244
  270.1 4.1 all-to-all-start.6
  274.2 1.7 convolution_select_fusion
  275.9 1.8 fusion.6
  277.7 1.7 copy.61
  279.4 13.7 %reduce.5 = f32[3072,64]{1,0:T(8,128)S(1)} reduce(f32[3072,1,64]{2,1,0:T(1,128)S(1)} %bitcast.178, f32[]{:T(128)} %broadcast.202), dimensions={1}, to_apply=%bitcast.148.reduce_sub_computation | reduce | bytes 1572868
  293.0 1.9 reshape.242
  294.9 6.5 %all-to-all-start.4 = ((f32[8,1,24576]{2,1,0:T(1,128)}), f32[8,1,24576]{2,1,0:T(1,128)S(1)}, u32[]{:S(2)}, u32[]{:S(2)}) async-start(f32[8,1,24576]{2,1,0:T(1,128)} %reshape.242), calls=%async_computation.4 | async-start | bytes 1572864 | tf_op jit(solution)/shard_map/all_to_all | solution.py:151
  301.4 2.5 reduce.8
  303.9 1.0 reshape.245
  305.7 1.5 fusion.30
  307.2 3.5 copy.68
  310.7 11.2 %all-to-all-done.4 = f32[8,1,24576]{2,1,0:T(1,128)S(1)} async-done(((f32[8,1,24576]{2,1,0:T(1,128)}), f32[8,1,24576]{2,1,0:T(1,128)S(1)}, u32[]{:S(2)}, u32[]{:S(2)}) %all-to-all-start.4) | async-done | bytes 786464 | tf_op jit(solution)/shard_map/all_to_all | solution.py:151
  321.9 0.9 copy-done.6
  322.8 3.8 all-to-all-start.7
  326.7 4.5 reduce.6
  331.2 4.2 reshape.243
  335.4 2.7 copy.62
  338.1 3.3 fusion.45
  341.4 3.6 copy.63
  345.0 52.5 %all-to-all-done.7 = f32[48,64,192]{2,1,0:T(8,128)S(1)} async-done(((f32[48,64,192]{2,1,0:T(8,128)}), f32[48,64,192]{2,1,0:T(8,128)S(1)}, u32[]{:S(2)}, u32[]{:S(2)}) %all-to-all-start.7) | async-done | bytes 2359328 | tf_op jit(solution)/shard_map/all_to_all | solution.py:175
  397.5 4.8 all-to-all-start.5
  402.3 3.5 copy.69
  405.8 4.3 broadcast_in_dim.68
  410.1 96.0 %all-to-all-done.5 = f32[48,64,384]{2,1,0:T(8,128)} async-done(((f32[48,64,384]{2,1,0:T(8,128)}), f32[48,64,384]{2,1,0:T(8,128)}, u32[]{:S(2)}, u32[]{:S(2)}) %all-to-all-start.5) | async-done | bytes 4718624 | tf_op jit(solution)/shard_map/all_to_all | solution.py:174
  506.1 7.2 %copy.64 = f32[6,64,8,384]{3,2,1,0:T(8,128)} copy(f32[6,64,8,384]{3,1,0,2:T(8,128)} %bitcast.44) | data formatting | bytes 9437184 | tf_op jit(solution)/shard_map/all_to_all | solution.py:174
  513.3 5.8 %broadcast_in_dim.66 = f32[1,6,64,3072]{3,2,1,0:T(8,128)} reshape(f32[6,64,8,384]{3,2,1,0:T(8,128)} %copy.64) | data formatting | bytes 9437184 | tf_op jit(solution)/shard_map/broadcast_in_dim | solution.py:177
  (90 shorter events, 10.8 us)
Async XLA Ops:
  7.2 1.3 copy-start.16
  7.2 231.6 %all-gather.3.cloned.1.call-start = ((), (), s32[]{:S(2)}) async-start(), calls=%async_computation.8 | async-start | bytes 10616832 | tf_op jit(solution)/shard_map/all_gather | solution.py:90
  17.0 7.5 %copy-start.7 = (bf16[1,6,64,3072]{3,2,1,0:T(8,128)(2,1)S(1)}, bf16[1,6,64,3072]{3,2,1,0:T(8,128)(2,1)}, u32[]{:S(2)}) copy-start(bf16[1,6,64,3072]{3,2,1,0:T(8,128)(2,1)} %param.16) | copy-start | bytes 7077892
  17.0 67.2 %all-to-all-start = ((bf16[8,2,36864]{2,1,0:T(2,128)(2,1)}), bf16[8,2,36864]{2,1,0:T(2,128)(2,1)S(1)}, u32[]{:S(2)}, u32[]{:S(2)}) async-start(bf16[8,2,36864]{2,1,0:T(2,128)(2,1)} %reshape.240), calls=%async_computation | async-start | bytes 2359296 | tf_op jit(solution)/shard_map/all_to_all | solution.py:104
  30.4 59.8 %copy-start.27 = (s32[48]{0:T(128)S(1)}, s32[48]{0:T(128)}, u32[]{:S(2)}) copy-start(s32[48]{0:T(128)} %param.19) | copy-start | bytes 580
  30.4 59.8 %copy-start.28 = (s32[8]{0:T(128)S(1)}, s32[8]{0:T(128)}, u32[]{:S(2)}) copy-start(s32[8]{0:T(128)} %param.18) | copy-start | bytes 100
  30.4 60.6 %copy-start.10 = (f32[128,3072]{1,0:T(8,128)S(1)}, f32[128,3072]{1,0:T(8,128)}, u32[]{:S(2)}) copy-start(f32[128,3072]{1,0:T(8,128)} %param.12) | copy-start | bytes 4718596
  84.2 1.0 copy-start.3
  85.2 115.8 %all-to-all-start.2 = ((bf16[8,6,64,384]{3,2,1,0:T(8,128)(2,1)}), bf16[8,6,64,384]{3,2,1,0:T(8,128)(2,1)}, u32[]{:S(2)}, u32[]{:S(2)}) async-start(bf16[8,6,64,384]{3,2,1,0:T(8,128)(2,1)} %fusion.35), calls=%async_computation.2 | async-start | bytes 4718592 | tf_op jit(solution)/shard_map/all_to_all | solution.py:99
  90.4 0.5 copy-start.24
  99.3 110.7 %copy-start = (bf16[128,3072]{1,0:T(8,128)(2,1)S(1)}, bf16[128,3072]{1,0:T(8,128)(2,1)}, u32[]{:S(2)}) copy-start(bf16[128,3072]{1,0:T(8,128)(2,1)} %param.11) | copy-start | bytes 2359300
  201.0 21.6 %all-to-all-start.1 = ((bf16[8,64,192]{2,1,0:T(8,128)(2,1)}), bf16[8,64,192]{2,1,0:T(8,128)(2,1)S(1)}, u32[]{:S(2)}, u32[]{:S(2)}) async-start(bf16[8,64,192]{2,1,0:T(8,128)(2,1)} %gather_fusion), calls=%async_computation.1 | async-start | bytes 524288 | tf_op jit(solution)/shard_map/all_to_all | solution.py:108
  210.0 2.8 copy-start.29
  211.9 14.2 %copy-start.1 = (f32[1,128,3072]{2,1,0:T(8,128)S(1)}, f32[1,128,3072]{2,1,0:T(8,128)}, u32[]{:S(2)}) copy-start(f32[1,128,3072]{2,1,0:T(8,128)} %get-tuple-element.7) | copy-start | bytes 4718596
  213.7 12.4 %copy-start.22 = (f32[128]{0:T(128)}, f32[128]{0:T(128)S(1)}, u32[]{:S(2)}) copy-start(f32[128]{0:T(128)S(1)} %fusion.20) | copy-start | bytes 1540
  222.6 3.5 copy-start.17
  222.6 14.8 %all-to-all-start.3 = ((bf16[8,64,384]{2,1,0:T(8,128)(2,1)}), bf16[8,64,384]{2,1,0:T(8,128)(2,1)S(1)}, u32[]{:S(2)}, u32[]{:S(2)}) async-start(bf16[8,64,384]{2,1,0:T(8,128)(2,1)} %gather_fusion.1), calls=%async_computation.3 | async-start | bytes 786432 | tf_op jit(solution)/shard_map/all_to_all | solution.py:107
  226.0 12.2 %copy-start.19 = (f32[1,3072]{1,0:T(1,128)S(1)}, f32[1,3072]{1,0:T(1,128)}, u32[]{:S(2)}) copy-start(f32[1,3072]{1,0:T(1,128)} %param.14) | copy-start | bytes 36868
  226.1 12.7 %copy-start.30 = (f32[128]{0:T(128)}, f32[128]{0:T(128)S(1)}, u32[]{:S(2)}) copy-start(f32[128]{0:T(128)S(1)} %add_rsqrt_fusion.1) | copy-start | bytes 1540
  229.8 17.2 %copy-start.8 = (bf16[64,1536]{1,0:T(8,128)(2,1)}, bf16[64,1536]{1,0:T(8,128)(2,1)S(1)}, u32[]{:S(2)}) copy-start(bf16[64,1536]{1,0:T(8,128)(2,1)S(1)} %reshape.213) | copy-start | bytes 589828
  237.5 0.7 copy-start.11
  238.7 5.4 %copy-start.18 = (bf16[128,64]{0,1:T(8,128)(2,1)}, bf16[128,64]{0,1:T(8,128)(2,1)S(1)}, u32[]{:S(2)}) copy-start(bf16[128,64]{0,1:T(8,128)(2,1)S(1)} %convolution_convert_fusion.1) | copy-start | bytes 49156
  238.8 5.3 %copy-start.5 = (f32[1,128,3072]{2,1,0:T(8,128)S(1)}, f32[1,128,3072]{2,1,0:T(8,128)}, u32[]{:S(2)}) copy-start(f32[1,128,3072]{2,1,0:T(8,128)} %get-tuple-element.9) | copy-start | bytes 4718596
  238.8 8.5 %copy-start.2 = (bf16[1,3072,1536]{2,1,0:T(8,128)(2,1)S(1)}, bf16[1,3072,1536]{2,1,0:T(8,128)(2,1)}, u32[]{:S(2)}) copy-start(bf16[1,3072,1536]{2,1,0:T(8,128)(2,1)} %all-gather.3.cloned.1.call-done) | copy-start | bytes 28311556
  244.1 1.5 copy-start.13
  245.7 4.7 collective-permute-start
  247.3 3.1 copy-start.12
  247.3 3.1 copy-start.20
  250.4 0.9 copy-start.23
  253.3 4.6 copy-start.4
  253.3 4.6 collective-permute-start.1
  259.7 0.7 copy-start.14
  261.6 12.5 %copy-start.9 = (bf16[64,1536]{1,0:T(8,128)(2,1)S(1)}, bf16[64,1536]{1,0:T(8,128)(2,1)}, u32[]{:S(2)}) copy-start(bf16[64,1536]{1,0:T(8,128)(2,1)} %copy-done.8) | copy-start | bytes 589828
  261.6 12.6 %copy-start.21 = (f32[1,3072]{1,0:T(1,128)S(1)}, f32[1,3072]{1,0:T(1,128)}, u32[]{:S(2)}) copy-start(f32[1,3072]{1,0:T(1,128)} %param.14) | copy-start | bytes 36868
  261.6 12.6 %copy-start.26 = (f32[128]{0:T(128)S(1)}, f32[128]{0:T(128)}, u32[]{:S(2)}) copy-start(f32[128]{0:T(128)} %get-tuple-element.11) | copy-start | bytes 1540
  261.6 12.6 %copy-start.31 = (f32[128]{0:T(128)S(1)}, f32[128]{0:T(128)}, u32[]{:S(2)}) copy-start(f32[128]{0:T(128)} %copy-done.30) | copy-start | bytes 1540
  268.8 5.4 %copy-start.15 = (bf16[128,1536]{1,0:T(8,128)(2,1)S(1)}, bf16[128,1536]{1,0:T(8,128)(2,1)}, u32[]{:S(2)}) copy-start(bf16[128,1536]{1,0:T(8,128)(2,1)} %copy-done.14) | copy-start | bytes 1179652
  270.1 24.8 %all-to-all-start.6 = ((f32[8,1,12288]{2,1,0:T(1,128)}), f32[8,1,12288]{2,1,0:T(1,128)}, u32[]{:S(2)}, u32[]{:S(2)}) async-start(f32[8,1,12288]{2,1,0:T(1,128)} %reshape.244), calls=%async_computation.6 | async-start | bytes 786432 | tf_op jit(solution)/shard_map/all_to_all | solution.py:152
  294.9 27.0 %all-to-all-start.4 = ((f32[8,1,24576]{2,1,0:T(1,128)}), f32[8,1,24576]{2,1,0:T(1,128)S(1)}, u32[]{:S(2)}, u32[]{:S(2)}) async-start(f32[8,1,24576]{2,1,0:T(1,128)} %reshape.242), calls=%async_computation.4 | async-start | bytes 1572864 | tf_op jit(solution)/shard_map/all_to_all | solution.py:151
  304.9 0.8 copy-start.25
  321.9 0.9 copy-start.6
  322.8 74.7 %all-to-all-start.7 = ((f32[48,64,192]{2,1,0:T(8,128)}), f32[48,64,192]{2,1,0:T(8,128)S(1)}, u32[]{:S(2)}, u32[]{:S(2)}) async-start(f32[48,64,192]{2,1,0:T(8,128)} %copy.68), calls=%async_computation.7 | async-start | bytes 6291456 | tf_op jit(solution)/shard_map/all_to_all | solution.py:175
  397.5 108.6 %all-to-all-start.5 = ((f32[48,64,384]{2,1,0:T(8,128)}), f32[48,64,384]{2,1,0:T(8,128)}, u32[]{:S(2)}, u32[]{:S(2)}) async-start(f32[48,64,384]{2,1,0:T(8,128)} %copy.63), calls=%async_computation.5 | async-start | bytes 9437184 | tf_op jit(solution)/shard_map/all_to_all | solution.py:174
Sparse Core Ops, SparseCore 0:
  10.2 214.9 all-gather.2
